TPU v7x, 256 devices: a whole 4x4x8 slice. The times are simulated.
256 devices in a mesh: chrom: 4 (over x), snp: 64 (over z, y, core).
Axes of the slice: x: 4, y: 4, z: 8, core: 2. Of those that a mesh axis runs over, the one named last changes fastest.
Arguments:
- genotypes: bfloat16 [12288, 131072], P(None, ('chrom', 'snp')), may hold values from 0 to 2, as said below
- probes: bfloat16 [131072, 128], P(('chrom', 'snp')), may hold values from -4 to 4
Outputs:
- unit_basis: float32 [131072, 128], P(('chrom', 'snp'))
- range_log_norms: float32 [128], replicated
Inputs may be any that keep to these rules, and one draw needn't show every extreme that they name: `genotypes`: every entry is a dosage 0, 1 or 2.
All inputs are finite; a program needn't handle non-finite values.
Results may differ from a plain program's by a relative error of at most 0.0034.
The roundings to bfloat16 on the way count: a program that leaves them out, or rounds other values in their place, can miss the bound.
Values sent between devices are 32-bit elements; how exact they have to be, the bound alone decides.
No kernel may reach another device: no remote copies, remote signals or barrier semaphores. Data moves between devices by JAX's collectives and lax.ppermute only.
A program may use at most 128 MiB of HBM per device.

v0:
```python
import functools
import math

import jax
import jax.numpy as jnp
from jax import lax
from jax.experimental import pallas as pl
from jax.experimental.pallas import tpu as pltpu
from jax.sharding import Mesh
from jax.sharding import PartitionSpec as P


AXES = ("x", "z", "y", "c")


def pair_list(sizes, move):
    nx, nz, ny, nc = sizes
    pairs = []
    for x in range(nx):
        for z in range(nz):
            for y in range(ny):
                for c in range(nc):
                    X, Z, Y, C = move(x, z, y, c)
                    src = ((x * nz + z) * ny + y) * nc + c
                    dst = (((X % nx) * nz + Z % nz) * ny + Y % ny) * nc + C % nc
                    pairs.append((src, dst))
    return pairs


class Torus:
    def __init__(self, sizes):
        self.sizes = sizes

    def core(self, value):
        return lax.ppermute(value, AXES, pair_list(self.sizes, lambda x, z, y, c: (x, z, y, c + 1)))

    def first(self, value, k):
        def move(x, z, y, c):
            return (x + k, z, y, c) if c == 0 else (x, z, y + k, c)

        return lax.ppermute(value, AXES, pair_list(self.sizes, move))

    def second(self, value, k):
        def move(x, z, y, c):
            return (x, z, y + k, c) if c == 0 else (x + k, z, y, c)

        return lax.ppermute(value, AXES, pair_list(self.sizes, move))

    def places(self):
        core, x, y = lax.axis_index("c"), lax.axis_index("x"), lax.axis_index("y")
        return core, jnp.where(core == 0, x, y), jnp.where(core == 0, y, x)


def add_pairs(a, b):
    total = a[0] + b[0]
    back = total - a[0]
    lost = (a[0] - (total - back)) + (b[0] - back)
    return jnp.stack([total, (a[1] + b[1]) + lost])


def sum_ring(value, send):
    got = [send(value, k) for k in (1, 2, 3)]
    return add_pairs(add_pairs(value, got[1]), add_pairs(got[0], got[2]))


def tree_sum(terms, add):
    while len(terms) > 1:
        terms = [add(*terms[i : i + 2]) for i in range(0, len(terms), 2)]
    return terms[0]


def sum_square(torus, kept, given):
    half = add_pairs(kept, torus.core(given))
    half = sum_ring(half, torus.first)
    half = sum_ring(half, torus.second)
    depth = torus.sizes[1]
    got = lax.all_to_all(jnp.broadcast_to(half, (depth, *half.shape)), "z", 0, 0)
    half = tree_sum([got[i] for i in range(depth)], add_pairs)
    return half, torus.core(half)


LIMIT = pltpu.CompilerParams(vmem_limit_bytes=20 * 2**20)
ONCHIP = pl.BlockSpec(memory_space=pltpu.VMEM)
SCALARS = pl.BlockSpec(memory_space=pltpu.SMEM)
SLICES = 5


def cut(values, peak):
    sigma = peak * 131072.0
    slices = []
    for _ in range(SLICES):
        part = (values + sigma) - sigma
        slices.append(part.astype(jnp.bfloat16))
        values = values - part
        sigma = sigma * 0.0078125
    return slices


def exact_gram(values, joined):
    flipped = values.T
    right = cut(values, jnp.max(jnp.abs(values), axis=0, keepdims=True))
    left = cut(flipped, jnp.max(jnp.abs(flipped), axis=1, keepdims=True))
    hi = jnp.zeros((values.shape[1], values.shape[1]), jnp.float32)
    lo = jnp.zeros_like(hi)
    for level in reversed(range(SLICES + 1)):
        picks = [i for i in range(SLICES) if 0 <= level - i < SLICES]
        for group in [picks] if joined else [[i] for i in picks]:
            term = jnp.dot(
                jnp.concatenate([left[i] for i in group], axis=1),
                jnp.concatenate([right[level - i] for i in group], axis=0),
                preferred_element_type=jnp.float32,
            )
            total = hi + term
            back = total - hi
            lo = lo + ((hi - (total - back)) + (term - back))
            hi = total
    return hi, lo


def pack(square):
    n = square.shape[0]
    row = lax.broadcasted_iota(jnp.int32, (n // 2, n), 0)
    col = lax.broadcasted_iota(jnp.int32, (n // 2, n), 1)
    last = pltpu.roll(square[n // 2 :], n // 2, 1)
    diagonal = jnp.sum(jnp.where(col == row, last, 0.0), axis=0, keepdims=True)
    tail = jnp.where(lax.broadcasted_iota(jnp.int32, (16, n), 0) == 0, diagonal, 0.0)
    return jnp.concatenate([jnp.where(col >= row, square[: n // 2], last), tail], axis=0)


def unpack(packed):
    n = packed.shape[1]
    row = lax.broadcasted_iota(jnp.int32, (n, n), 0)
    col = lax.broadcasted_iota(jnp.int32, (n, n), 1)
    diagonal = pltpu.roll(packed[n // 2 : n // 2 + 8], n // 2, 1)[0:1]
    whole = jnp.concatenate([packed[: n // 2], jnp.zeros((n // 2, n), jnp.float32)], axis=0)
    flipped = whole.T
    low = pltpu.roll(pltpu.roll(whole, n // 2, 0), n // 2, 1)
    low_flipped = pltpu.roll(pltpu.roll(flipped, n // 2, 0), n // 2, 1)
    last = jnp.where(col < row, low, jnp.where(col == row, diagonal, low_flipped))
    below = jnp.where(col < n // 2, flipped, last)
    return jnp.where(row < n // 2, jnp.where(col >= row, whole, flipped), below)


def gram_kernel(table_ref, range_ref, kept_ref, given_ref):
    rows = kept_ref.shape[1]
    first = table_ref[12] == 0
    for i, square in enumerate(exact_gram(range_ref[...].T, False)):
        packed = pack(square)
        kept_ref[i] = jnp.where(first, packed[:rows], packed[rows:])
        given_ref[i] = jnp.where(first, packed[rows:], packed[:rows])


def exact_dot(a, b):
    return lax.dot_general(
        a,
        b,
        (((1,), (0,)), ((), ())),
        precision=lax.Precision.HIGHEST,
        preferred_element_type=jnp.float32,
    )


def short_dot(a, b):
    a, b = a.astype(jnp.bfloat16), b.astype(jnp.bfloat16)
    return jnp.dot(a, b, preferred_element_type=jnp.float32)


def eliminate(matrix, a_ref, b_ref):
    n = matrix.shape[0]
    row = lax.broadcasted_iota(jnp.int32, (n, n), 0)
    col = lax.broadcasted_iota(jnp.int32, (n, n), 1)
    a_ref[...] = matrix
    b_ref[...] = (row == col).astype(jnp.float32)
    column_row = lax.broadcasted_iota(jnp.int32, (n, 1), 0)
    panel_row = lax.broadcasted_iota(jnp.int32, (8, 1), 0)

    def block(index, carry):
        start = pl.multiple_of(index * 8, 8)
        a, b = a_ref[...], b_ref[...]
        pa, pb = a_ref[pl.ds(start, 8), :], b_ref[pl.ds(start, 8), :]
        after = column_row >= start + 8
        for t in range(8):
            lane = jnp.broadcast_to(pa[:, t : t + 1], (8, n))
            inverse = 1.0 / lane[t : t + 1]
            ra, rb = pa[t : t + 1], pb[t : t + 1]
            if t < 7:
                masked = jnp.where(panel_row > t, lane, 0.0)
                pa, pb = pa - (masked * ra) * inverse, pb - (masked * rb) * inverse
            factor = jnp.where(after, a[:, t : t + 1], 0.0)
            a, b = a - (factor * ra) * inverse, b - factor * (rb * inverse)
        a_ref[...] = pltpu.roll(a, n - 8, 1)
        b_ref[...] = b
        a_ref[pl.ds(start, 8), :] = pltpu.roll(pa, n - 8, 1)
        b_ref[pl.ds(start, 8), :] = pb
        return carry

    lax.fori_loop(0, n // 8, block, 0)
    upper = jnp.where(col >= row, a_ref[...], 0.0)
    pivot = jnp.sum(jnp.where(col == row, upper, 0.0), axis=1, keepdims=True)
    root = lax.rsqrt(pivot)
    return upper * root, b_ref[...] * root


def factor_kernel(scale, count, table_ref, half_ref, other_ref, basis_ref, norms_ref, a_ref, b_ref, out_ref):
    first = table_ref[12] == 0
    squares = []
    for i in range(2):
        above = jnp.where(first, half_ref[i], other_ref[i])
        below = jnp.where(first, other_ref[i], half_ref[i])
        squares.append(unpack(jnp.concatenate([above, below], axis=0)))
    hi, lo = squares
    n = hi.shape[0]
    row = lax.broadcasted_iota(jnp.int32, (n, n), 0)
    col = lax.broadcasted_iota(jnp.int32, (n, n), 1)
    eye = row == col
    total = hi + lo
    lo = (hi - total) + lo
    hi = total
    diagonal = jnp.sum(jnp.where(eye, hi, 0.0), axis=0, keepdims=True)
    norms_ref[...] = 0.1 * jnp.log(diagonal / count)
    upper, below = eliminate(hi, a_ref, b_ref)
    back_hi, back_lo = exact_gram(upper, True)
    rest = ((hi - back_hi) - back_lo) + lo
    above = below.T
    rest = exact_dot(exact_dot(below, rest), above)
    size = jnp.sum(rest * rest)

    @pl.when(size < 0.002)
    def _():
        half = jnp.where(eye, 0.5, jnp.where(col > row, 1.0, 0.0))
        step = half * rest
        for _ in range(3):
            step = half * (rest - short_dot(step.T, step))
        square = short_dot(step, step)
        inverse = eye.astype(jnp.float32) - step
        inverse = inverse + short_dot(inverse, square)
        out_ref[...] = inverse + short_dot(inverse, short_dot(square, square))

    @pl.when(jnp.logical_not(size < 0.002))
    def _():
        _, small = eliminate(eye.astype(jnp.float32) + rest, a_ref, b_ref)
        out_ref[...] = small.T

    basis_ref[...] = scale * exact_dot(above, out_ref[...])


def local_gram(table, range_columns):
    width = range_columns.shape[0]
    return pl.pallas_call(
        gram_kernel,
        in_specs=[SCALARS, ONCHIP],
        out_specs=[ONCHIP] * 2,
        out_shape=[jax.ShapeDtypeStruct((2, width // 4 + 8, width), jnp.float32)] * 2,
        compiler_params=LIMIT,
        name="local_gram",
    )(table, range_columns)


def two_factors(table, half, other, total_snps):
    width = half.shape[2]
    return pl.pallas_call(
        functools.partial(factor_kernel, math.sqrt(total_snps), float(total_snps)),
        in_specs=[SCALARS] + [ONCHIP] * 2,
        out_shape=(
            jax.ShapeDtypeStruct((width, width), jnp.float32),
            jax.ShapeDtypeStruct((1, width), jnp.float32),
        ),
        scratch_shapes=[pltpu.VMEM((width, width), jnp.float32)] * 3,
        compiler_params=LIMIT,
        name="two_factors",
    )(table, half, other)


STEPS = 3
CHUNKS = 16


def resident(shape, dtype=jnp.float32):
    return pltpu.VMEM(shape, dtype)


def onchip(value):
    return pltpu.with_memory_space_constraint(value, pltpu.VMEM)


def offchip(value):
    return pltpu.with_memory_space_constraint(value, pltpu.HBM)


def stats_kernel(table_ref, source_ref, held_ref, out_ref, sems):
    samples, width = source_ref.shape
    rows = samples // CHUNKS

    def copy(i):
        part = pl.ds(pl.multiple_of(i * rows, rows), rows)
        return pltpu.make_async_copy(source_ref.at[part], held_ref.at[part], sems.at[i])

    for i in range(CHUNKS):
        copy(i).start()

    def add(i, sums):
        copy(i).wait()
        values = held_ref[pl.ds(pl.multiple_of(i * rows, rows), rows), :].astype(jnp.float32)
        values = values.reshape(rows // 8, 8, width)
        return sums[0] + jnp.sum(values, axis=0), sums[1] + jnp.sum(values * values, axis=0)

    zero = jnp.zeros((8, width), jnp.float32)
    first, square = lax.fori_loop(0, CHUNKS, add, (zero, zero))
    first = jnp.sum(first, axis=0, keepdims=True)
    square = jnp.sum(square, axis=0, keepdims=True)
    whole = first.astype(jnp.int32)
    exact = samples * square.astype(jnp.int32) - whole * whole
    spread = exact.astype(jnp.float32) / float(samples * samples)
    out_ref[0:1] = first / float(samples)
    out_ref[1:2] = lax.rsqrt(jnp.sqrt(jnp.sqrt(spread + 1e-05)))


def dosage_stats(table, genotypes):
    samples, width = genotypes.shape
    return pl.pallas_call(
        stats_kernel,
        in_specs=[SCALARS, pl.BlockSpec(memory_space=pltpu.HBM)],
        out_specs=[ONCHIP] * 2,
        out_shape=[resident((samples, width), genotypes.dtype), resident((2, width))],
        scratch_shapes=[pltpu.SemaphoreType.DMA((CHUNKS,))],
        compiler_params=LIMIT,
        name="dosage_stats",
    )(table, offchip(genotypes))


def scaled_rows(held_ref, stats_ref, start, rows):
    dosages = held_ref[pl.ds(pl.multiple_of(start, rows), rows), :].astype(jnp.float32)
    return ((dosages - stats_ref[0:1]) * stats_ref[1:2]).astype(jnp.bfloat16)


def sum_kernel(table_ref, zero_ref, one_ref, two_ref, three_ref, *out_refs):
    rows = out_refs[0].shape[0]
    for k, out_ref in enumerate(out_refs):
        part = pl.ds(pl.multiple_of(table_ref[8 + k] * rows, rows), rows)
        out_ref[...] = (zero_ref[part] + two_ref[part]) + (one_ref[part] + three_ref[part])


def sum_quarter(table, got):
    rows, width = got[0].shape
    return pl.pallas_call(
        sum_kernel,
        in_specs=[SCALARS] + [ONCHIP] * 4,
        out_specs=[ONCHIP] * 4,
        out_shape=[resident((rows // 4, width))] * 4,
        compiler_params=LIMIT,
        name="sum_quarter",
    )(table, *(onchip(got[k]) for k in range(4)))


def join_kernel(table_ref, *refs):
    *part_refs, out_ref = refs
    rows = part_refs[0].shape[0]
    for k, part_ref in enumerate(part_refs):
        start = pl.multiple_of(table_ref[8 + (4 - k) % 4] * rows, rows)
        out_ref[pl.ds(start, rows)] = part_ref[...]


def join_quarter(table, parts):
    rows, width = parts[0].shape
    return pl.pallas_call(
        join_kernel,
        in_specs=[SCALARS] + [ONCHIP] * 4,
        out_specs=ONCHIP,
        out_shape=resident((4 * rows, width)),
        compiler_params=LIMIT,
        name="join_quarter",
    )(table, *(onchip(part) for part in parts))


def sketch_kernel(k, table_ref, held_ref, stats_ref, probes_ref, kept_ref, given_ref):
    whole = kept_ref.shape[0]
    rows = whole // STEPS

    def step(i, carry):
        part = pl.ds(pl.multiple_of(i * rows, rows), rows)
        for slot, target in ((4 + k, given_ref), (k, kept_ref)):
            scaled = scaled_rows(held_ref, stats_ref, table_ref[slot] * whole + i * rows, rows)
            target[part, :] = jnp.dot(scaled, probes_ref[...], preferred_element_type=jnp.float32)
        return carry

    lax.fori_loop(0, STEPS, step, 0)


def sketch_piece(k, table, held, stats, probes):
    samples, snps = held.shape
    width = probes.shape[1]
    return pl.pallas_call(
        functools.partial(sketch_kernel, k),
        in_specs=[SCALARS, ONCHIP, ONCHIP, ONCHIP],
        out_specs=[ONCHIP] * 2,
        out_shape=[resident((samples // 8, width))] * 2,
        compiler_params=LIMIT,
        cost_estimate=pl.CostEstimate(
            flops=samples // 2 * snps * width, transcendentals=0, bytes_accessed=samples * snps // 2
        ),
        name="sketch_piece",
    )(table, held, stats, probes)


def range_kernel(slots, table_ref, held_ref, stats_ref, acc_ref, *refs):
    *sketch_refs, out_ref = refs
    width = acc_ref.shape[0]
    whole = sketch_refs[0].shape[0]
    rows = whole // STEPS
    out_ref[...] = acc_ref[...]

    def step(i, carry):
        part = pl.ds(pl.multiple_of(i * rows, rows), rows)
        for slot, sketch_ref in zip(slots, sketch_refs):
            sketch = sketch_ref[part, :].T
            high = sketch.astype(jnp.bfloat16)
            rest = sketch - high.astype(jnp.float32)
            mid = rest.astype(jnp.bfloat16)
            low = (rest - mid.astype(jnp.float32)).astype(jnp.bfloat16)
            parts = jnp.concatenate([high, mid, low], axis=0)
            scaled = scaled_rows(held_ref, stats_ref, table_ref[slot] * whole + i * rows, rows)
            product = jnp.dot(parts, scaled, preferred_element_type=jnp.float32)
            out_ref[...] += product[:width] + product[width : 2 * width] + product[2 * width :]
        return carry

    lax.fori_loop(0, STEPS, step, 0)


def range_piece(slots, table, held, stats, acc, *sketches):
    samples, snps = held.shape
    width = acc.shape[0]
    part = samples // 8 * len(slots)
    return pl.pallas_call(
        functools.partial(range_kernel, slots),
        in_specs=[SCALARS] + [ONCHIP] * (3 + len(slots)),
        out_specs=ONCHIP,
        out_shape=resident((width, snps)),
        compiler_params=LIMIT,
        cost_estimate=pl.CostEstimate(
            flops=6 * part * snps * width, transcendentals=0, bytes_accessed=2 * part * snps
        ),
        name="range_piece",
    )(table, held, stats, acc, *(onchip(sketch) for sketch in sketches))


def solution(mesh):
    nx = mesh.shape["chrom"]
    nz = mesh.shape["snp"] // 8
    torus = Torus((nx, nz, 4, 2))
    fine = Mesh(mesh.devices.reshape(torus.sizes), AXES)

    def body(genotypes, probes):
        samples, snps = genotypes.shape
        width = probes.shape[1]
        total_snps = snps * fine.size
        core, one, two = torus.places()
        turns = jnp.arange(4, dtype=jnp.int32)
        table = jnp.concatenate(
            [
                core * 4 + ((one + turns) & 3),
                (1 - core) * 4 + ((two + turns) & 3),
                (two + turns) & 3,
                core[None],
            ]
        ).astype(jnp.int32)
        held, stats = (onchip(v) for v in dosage_stats(table, genotypes))
        got = {}
        for k in (2, 1, 3, 0):
            kept, given = sketch_piece(k, table, held, stats, probes)
            piece = kept + torus.core(given)
            got[k] = torus.first(piece, k) if k else piece
        split = sum_quarter(table, got)
        got = [torus.second(split[k], k) for k in (1, 2, 3)]
        small = (split[0] + got[1]) + (got[0] + got[2])
        small = small.reshape(nz, samples // 32 // nz, width)
        own = lax.all_to_all(small, "z", 0, 0)
        own = tree_sum([own[i] for i in range(nz)], jnp.add)
        small = lax.all_to_all(jnp.broadcast_to(own, (nz, *own.shape)), "z", 0, 0)
        small = small.reshape(samples // 32, width)
        quarter = join_quarter(table, [small] + [torus.second(small, k) for k in (1, 2, 3)])
        mine = {0: quarter}
        for k in (1, 3, 2):
            mine[k] = torus.first(quarter, k)
        acc = jnp.zeros((width, snps), jnp.float32)
        acc = range_piece((0,), table, held, stats, acc, quarter)
        for k in (0, 1, 3, 2):
            slot = (4 - k) % 4
            theirs = torus.core(mine[k])
            if k:
                acc = range_piece((slot, 4 + slot), table, held, stats, acc, mine[k], theirs)
            else:
                acc = range_piece((4,), table, held, stats, acc, theirs)
        half, other = sum_square(torus, *local_gram(table, acc))
        basis, range_log_norms = two_factors(table, half, other, total_snps)
        unit_basis = lax.dot_general(
            acc,
            basis,
            (((0,), (0,)), ((), ())),
            precision=lax.Precision.HIGHEST,
            preferred_element_type=jnp.float32,
        )
        return (unit_basis, range_log_norms[0])

    return jax.shard_map(
        body,
        mesh=fine,
        in_specs=(P(None, AXES), P(AXES, None)),
        out_specs=(P(AXES, None), P()),
        check_vma=False,
    )
```

profile of v0, /device:TPU:1, one launch (start us, length us, event | category | flops | bytes accessed | tf_op | source)
XLA Modules:
  0.0 178.7 jit_solution(9597477576991958960)
XLA Ops:
  0.8 5.4 %dosage_stats.1 = (bf16[12288,512]{1,0:T(8,128)(2,1)S(1)}, f32[2,512]{1,0:T(2,128)S(1)}) custom-call(s32[13]{0:T(128)S(1)} %pad_add_fusion.table_ref, bf16[12288,512]{1,0:T(8,128)(2,1)} %source_ref.1), custom_call_target="tpu_custom_call" | custom-call | tf_op jit(solution)/shard_map/dosage_stats/pallas_call | solution.py:320
  6.2 1.9 %sketch_piece.7 = (f32[1536,128]{1,0:T(8,128)S(1)}, f32[1536,128]{1,0:T(8,128)S(1)}) custom-call(s32[13]{0:T(128)S(1)} %pad_add_fusion.table_ref, bf16[12288,512]{1,0:T(8,128)(2,1)S(1)} %get-tuple-element.20.held_ref, f32[2,512]{1,0:T(2,128)S(1)} %get-tuple-element.21.stats_ref, bf16[512,128]{1,0:T(8,128)(2,1)S(1)} %copy-done), custom_call_target="tpu_custom_call" | custom-call | flops 402653184 | bytes 3145728 | tf_op jit(solution)/shard_map/sketch_piece/pallas_call | solution.py:392
  8.1 3.3 %collective-permute-start.5 = (f32[1536,128]{1,0:T(8,128)S(1)}, f32[1536,128]{1,0:T(8,128)S(1)}, u32[]{:S(2)}, u32[]{:S(2)}) collective-permute-start(f32[1536,128]{1,0:T(8,128)S(1)} %get-tuple-element.29), channel_id=1, source_target_pairs={{0,1},{1,0},{2,3},{3,2},{4,5},{5,4},{6,7},{7,6},{8,9},{9,8},{10,11... | collective-permute-start | bytes 2359304 | tf_op jit(solution)/shard_map/ppermute | solution.py:35
  20.6 8.6 %collective-permute-done.6.three_ref = f32[1536,128]{1,0:T(8,128)S(1)} collective-permute-done((f32[1536,128]{1,0:T(8,128)S(1)}, f32[1536,128]{1,0:T(8,128)S(1)}, u32[]{:S(2)}, u32[]{:S(2)}) %collective-permute-start.6) | collective-permute-done | bytes 786464 | tf_op jit(solution)/shard_map/ppermute | solution.py:41
  29.2 2.8 %collective-permute-done.4.two_ref = f32[1536,128]{1,0:T(8,128)S(1)} collective-permute-done((f32[1536,128]{1,0:T(8,128)S(1)}, f32[1536,128]{1,0:T(8,128)S(1)}, u32[]{:S(2)}, u32[]{:S(2)}) %collective-permute-start.4) | collective-permute-done | bytes 786464 | tf_op jit(solution)/shard_map/ppermute | solution.py:41
  32.0 8.4 %collective-permute-done.2.one_ref = f32[1536,128]{1,0:T(8,128)S(1)} collective-permute-done((f32[1536,128]{1,0:T(8,128)S(1)}, f32[1536,128]{1,0:T(8,128)S(1)}, u32[]{:S(2)}, u32[]{:S(2)}) %collective-permute-start.2) | collective-permute-done | bytes 786464 | tf_op jit(solution)/shard_map/ppermute | solution.py:41
  41.1 2.5 %collective-permute-start.7 = (f32[384,128]{1,0:T(8,128)S(1)}, f32[384,128]{1,0:T(8,128)S(1)}, u32[]{:S(2)}, u32[]{:S(2)}) collective-permute-start(f32[384,128]{1,0:T(8,128)S(1)} %get-tuple-element.31), channel_id=1, source_target_pairs={{0,4},{1,129},{2,6},{3,131},{4,0},{5,133},{6,2},{7,135},{8,12},{9,... | collective-permute-start | bytes 589832 | tf_op jit(solution)/shard_map/ppermute | solution.py:47
  44.0 2.4 %collective-permute-start.9 = (f32[384,128]{1,0:T(8,128)S(1)}, f32[384,128]{1,0:T(8,128)S(1)}, u32[]{:S(2)}, u32[]{:S(2)}) collective-permute-start(f32[384,128]{1,0:T(8,128)S(1)} %get-tuple-element.33), channel_id=1, source_target_pairs={{0,6},{1,193},{2,0},{3,195},{4,2},{5,197},{6,4},{7,199},{8,14},{9,... | collective-permute-start | bytes 589832 | tf_op jit(solution)/shard_map/ppermute | solution.py:47
  49.4 16.7 %all_to_all.15 = f32[8,48,128]{2,1,0:T(8,128)S(1)} all-to-all(f32[8,48,128]{2,1,0:T(8,128)S(1)} %bitcast.126), channel_id=1, replica_groups=mesh['x'=4,'z'=8,'y'=4,'c'=2] {'z'}, dimensions={0} | all-to-all | bytes 393216 | tf_op jit(solution)/shard_map/all_to_all | solution.py:476
  66.2 11.0 %all_to_all.16 = f32[8,48,128]{2,1,0:T(8,128)S(1)} all-to-all(f32[8,48,128]{2,1,0:T(8,128)S(1)} %broadcast_in_dim.14), channel_id=1, replica_groups=mesh['x'=4,'z'=8,'y'=4,'c'=2] {'z'}, dimensions={0} | all-to-all | bytes 393216 | tf_op jit(solution)/shard_map/all_to_all | solution.py:478
  78.5 3.6 %collective-permute-start.11 = (f32[384,128]{1,0:T(8,128)S(1)}, f32[384,128]{1,0:T(8,128)S(1)}, u32[]{:S(2)}, u32[]{:S(2)}) collective-permute-start(f32[384,128]{1,0:T(8,128)S(1)} %bitcast.123), channel_id=1, source_target_pairs={{0,4},{1,129},{2,6},{3,131},{4,0},{5,133},{6,2},{7,135},{8,12},{9,... | collective-permute-start | bytes 589832 | tf_op jit(solution)/shard_map/ppermute | solution.py:47
  84.0 3.3 %collective-permute-done.11.refs_2_ = f32[384,128]{1,0:T(8,128)S(1)} collective-permute-done((f32[384,128]{1,0:T(8,128)S(1)}, f32[384,128]{1,0:T(8,128)S(1)}, u32[]{:S(2)}, u32[]{:S(2)}) %collective-permute-start.11) | collective-permute-done | bytes 196640 | tf_op jit(solution)/shard_map/ppermute | solution.py:47
  88.0 2.7 %collective-permute-start.16 = (f32[1536,128]{1,0:T(8,128)S(1)}, f32[1536,128]{1,0:T(8,128)S(1)}, u32[]{:S(2)}, u32[]{:S(2)}) collective-permute-start(f32[1536,128]{1,0:T(8,128)S(1)} %join_quarter.1.refs_0_), channel_id=1, source_target_pairs={{0,192},{1,7},{2,194},{3,1},{4,196},{5,3},{6,198},{7,5},{8,200},{9... | collective-permute-start | bytes 2359304 | tf_op jit(solution)/shard_map/ppermute | solution.py:41
  90.6 9.7 %collective-permute-start.13 = (f32[1536,128]{1,0:T(8,128)S(1)}, f32[1536,128]{1,0:T(8,128)S(1)}, u32[]{:S(2)}, u32[]{:S(2)}) collective-permute-start(f32[1536,128]{1,0:T(8,128)S(1)} %join_quarter.1.refs_0_), channel_id=1, source_target_pairs={{0,1},{1,0},{2,3},{3,2},{4,5},{5,4},{6,7},{7,6},{8,9},{9,8},{10,11... | collective-permute-start | bytes 2359304 | tf_op jit(solution)/shard_map/ppermute | solution.py:35
  100.4 10.4 %collective-permute-done.14.refs_0_ = f32[1536,128]{1,0:T(8,128)S(1)} collective-permute-done((f32[1536,128]{1,0:T(8,128)S(1)}, f32[1536,128]{1,0:T(8,128)S(1)}, u32[]{:S(2)}, u32[]{:S(2)}) %collective-permute-start.14) | collective-permute-done | bytes 786464 | tf_op jit(solution)/shard_map/ppermute | solution.py:41
  110.8 7.9 %collective-permute-start.15 = (f32[1536,128]{1,0:T(8,128)S(1)}, f32[1536,128]{1,0:T(8,128)S(1)}, u32[]{:S(2)}, u32[]{:S(2)}) collective-permute-start(f32[1536,128]{1,0:T(8,128)S(1)} %collective-permute-done.14.refs_0_), channel_id=1, source_target_pairs={{0,1},{1,0},{2,3},{3,2},{4,5},{5,4},{6,7},{7,6},{8,9},{9,8},{10,11... | collective-permute-start | bytes 2359304 | tf_op jit(solution)/shard_map/ppermute | solution.py:35
  122.9 2.5 %range_piece.7.acc_ref = f32[128,512]{1,0:T(8,128)S(1)} custom-call(s32[13]{0:T(128)S(1)} %pad_add_fusion.table_ref, bf16[12288,512]{1,0:T(8,128)(2,1)S(1)} %get-tuple-element.20.held_ref, f32[2,512]{1,0:T(2,128)S(1)} %get-tuple-element.21.stats_ref, f32[128,512]{1,0:T(8,128)S(1)} %range_piece.6.acc_ref, f32[1536,128]{1,0:T(8,128)S(1)} %collective-permute-done.14.refs_0_, ...), custom_call_target="tpu_custom_call" | custom-call | flops 1207959552 | bytes 3145728 | tf_op jit(solution)/shard_map/range_piece/pallas_call | solution.py:433
  125.4 2.5 %range_piece.8.acc_ref = f32[128,512]{1,0:T(8,128)S(1)} custom-call(s32[13]{0:T(128)S(1)} %pad_add_fusion.table_ref, bf16[12288,512]{1,0:T(8,128)(2,1)S(1)} %get-tuple-element.20.held_ref, f32[2,512]{1,0:T(2,128)S(1)} %get-tuple-element.21.stats_ref, f32[128,512]{1,0:T(8,128)S(1)} %range_piece.7.acc_ref, f32[1536,128]{1,0:T(8,128)S(1)} %collective-permute-done.16.refs_0_, ...), custom_call_target="tpu_custom_call" | custom-call | flops 1207959552 | bytes 3145728 | tf_op jit(solution)/shard_map/range_piece/pallas_call | solution.py:433
  127.9 2.5 %range_piece.9.range_ref = f32[128,512]{1,0:T(8,128)S(1)} custom-call(s32[13]{0:T(128)S(1)} %pad_add_fusion.table_ref, bf16[12288,512]{1,0:T(8,128)(2,1)S(1)} %get-tuple-element.20.held_ref, f32[2,512]{1,0:T(2,128)S(1)} %get-tuple-element.21.stats_ref, f32[128,512]{1,0:T(8,128)S(1)} %range_piece.8.acc_ref, f32[1536,128]{1,0:T(8,128)S(1)} %collective-permute-done.18.refs_0_, ...), custom_call_target="tpu_custom_call" | custom-call | flops 1207959552 | bytes 3145728 | tf_op jit(solution)/shard_map/range_piece/pallas_call | solution.py:433
  133.8 2.7 %collective-permute-start.23 = (f32[2,40,128]{2,1,0:T(8,128)S(1)}, f32[2,40,128]{2,1,0:T(8,128)S(1)}, u32[]{:S(2)}, u32[]{:S(2)}) collective-permute-start(f32[2,40,128]{2,1,0:T(8,128)S(1)} %pad_maximum_fusion), channel_id=1, source_target_pairs={{0,192},{1,7},{2,194},{3,1},{4,196},{5,3},{6,198},{7,5},{8,200},{9... | collective-permute-start | bytes 122888 | tf_op jit(solution)/shard_map/ppermute | solution.py:41
  138.7 2.9 %collective-permute-start.25 = (f32[2,40,128]{2,1,0:T(8,128)S(1)}, f32[2,40,128]{2,1,0:T(8,128)S(1)}, u32[]{:S(2)}, u32[]{:S(2)}) collective-permute-start(f32[2,40,128]{2,1,0:T(8,128)S(1)} %pad_maximum_fusion.1), channel_id=1, source_target_pairs={{0,2},{1,65},{2,4},{3,67},{4,6},{5,69},{6,0},{7,71},{8,10},{9,73},... | collective-permute-start | bytes 122888 | tf_op jit(solution)/shard_map/ppermute | solution.py:47
  144.5 12.4 %all_to_all.17 = f32[8,2,40,128]{3,2,1,0:T(8,128)S(1)} all-to-all(f32[8,2,40,128]{3,2,1,0:T(8,128)S(1)} %broadcast_in_dim.15), channel_id=1, replica_groups=mesh['x'=4,'z'=8,'y'=4,'c'=2] {'z'}, dimensions={0} | all-to-all | bytes 655360 | tf_op jit(solution)/shard_map/all_to_all | solution.py:77
  157.0 4.6 %collective-permute-start.27 = (f32[2,40,128]{2,1,0:T(8,128)S(1)}, f32[2,40,128]{2,1,0:T(8,128)S(1)}, u32[]{:S(2)}, u32[]{:S(2)}) collective-permute-start(f32[2,40,128]{2,1,0:T(8,128)S(1)} %pad_maximum_fusion.3.half_ref), channel_id=1, source_target_pairs={{0,1},{1,0},{2,3},{3,2},{4,5},{5,4},{6,7},{7,6},{8,9},{9,8},{10,11... | collective-permute-start | bytes 122888 | tf_op jit(solution)/shard_map/ppermute | solution.py:35
  162.5 14.8 %two_factors.1 = (f32[128,128]{1,0:T(8,128)S(1)}, f32[1,128]{1,0:T(1,128)}) custom-call(s32[13]{0:T(128)S(1)} %pad_add_fusion.table_ref, f32[2,40,128]{2,1,0:T(8,128)S(1)} %pad_maximum_fusion.3.half_ref, f32[2,40,128]{2,1,0:T(8,128)S(1)} %collective-permute-done.27.other_ref), custom_call_target="tpu_custom_call" | custom-call | tf_op jit(solution)/shard_map/two_factors/pallas_call | solution.py:261
  (73 shorter events, 32.2 us)
Async XLA Ops:
  8.1 9.8 %collective-permute-start.5 = (f32[1536,128]{1,0:T(8,128)S(1)}, f32[1536,128]{1,0:T(8,128)S(1)}, u32[]{:S(2)}, u32[]{:S(2)}) collective-permute-start(f32[1536,128]{1,0:T(8,128)S(1)} %get-tuple-element.29), channel_id=1, source_target_pairs={{0,1},{1,0},{2,3},{3,2},{4,5},{5,4},{6,7},{7,6},{8,9},{9,8},{10,11... | collective-permute-start | bytes 2359304 | tf_op jit(solution)/shard_map/ppermute | solution.py:35
  13.3 5.8 %collective-permute-start.3 = (f32[1536,128]{1,0:T(8,128)S(1)}, f32[1536,128]{1,0:T(8,128)S(1)}, u32[]{:S(2)}, u32[]{:S(2)}) collective-permute-start(f32[1536,128]{1,0:T(8,128)S(1)} %get-tuple-element.27), channel_id=1, source_target_pairs={{0,1},{1,0},{2,3},{3,2},{4,5},{5,4},{6,7},{7,6},{8,9},{9,8},{10,11... | collective-permute-start | bytes 2359304 | tf_op jit(solution)/shard_map/ppermute | solution.py:35
  18.0 11.2 %collective-permute-start.6 = (f32[1536,128]{1,0:T(8,128)S(1)}, f32[1536,128]{1,0:T(8,128)S(1)}, u32[]{:S(2)}, u32[]{:S(2)}) collective-permute-start(f32[1536,128]{1,0:T(8,128)S(1)} %add.552), channel_id=1, source_target_pairs={{0,192},{1,7},{2,194},{3,1},{4,196},{5,3},{6,198},{7,5},{8,200},{9... | collective-permute-start | bytes 2359304 | tf_op jit(solution)/shard_map/ppermute | solution.py:41
  19.2 12.8 %collective-permute-start.4 = (f32[1536,128]{1,0:T(8,128)S(1)}, f32[1536,128]{1,0:T(8,128)S(1)}, u32[]{:S(2)}, u32[]{:S(2)}) collective-permute-start(f32[1536,128]{1,0:T(8,128)S(1)} %add.551), channel_id=1, source_target_pairs={{0,128},{1,5},{2,130},{3,7},{4,132},{5,1},{6,134},{7,3},{8,136},{9... | collective-permute-start | bytes 2359304 | tf_op jit(solution)/shard_map/ppermute | solution.py:41
  19.7 20.6 %collective-permute-start.2 = (f32[1536,128]{1,0:T(8,128)S(1)}, f32[1536,128]{1,0:T(8,128)S(1)}, u32[]{:S(2)}, u32[]{:S(2)}) collective-permute-start(f32[1536,128]{1,0:T(8,128)S(1)} %add.550), channel_id=1, source_target_pairs={{0,64},{1,3},{2,66},{3,5},{4,68},{5,7},{6,70},{7,1},{8,72},{9,11},... | collective-permute-start | bytes 2359304 | tf_op jit(solution)/shard_map/ppermute | solution.py:41
  41.1 6.4 %collective-permute-start.7 = (f32[384,128]{1,0:T(8,128)S(1)}, f32[384,128]{1,0:T(8,128)S(1)}, u32[]{:S(2)}, u32[]{:S(2)}) collective-permute-start(f32[384,128]{1,0:T(8,128)S(1)} %get-tuple-element.31), channel_id=1, source_target_pairs={{0,4},{1,129},{2,6},{3,131},{4,0},{5,133},{6,2},{7,135},{8,12},{9,... | collective-permute-start | bytes 589832 | tf_op jit(solution)/shard_map/ppermute | solution.py:47
  43.6 5.7 %collective-permute-start.8 = (f32[384,128]{1,0:T(8,128)S(1)}, f32[384,128]{1,0:T(8,128)S(1)}, u32[]{:S(2)}, u32[]{:S(2)}) collective-permute-start(f32[384,128]{1,0:T(8,128)S(1)} %get-tuple-element.32), channel_id=1, source_target_pairs={{0,2},{1,65},{2,4},{3,67},{4,6},{5,69},{6,0},{7,71},{8,10},{9,73},... | collective-permute-start | bytes 589832 | tf_op jit(solution)/shard_map/ppermute | solution.py:47
  44.0 5.4 %collective-permute-start.9 = (f32[384,128]{1,0:T(8,128)S(1)}, f32[384,128]{1,0:T(8,128)S(1)}, u32[]{:S(2)}, u32[]{:S(2)}) collective-permute-start(f32[384,128]{1,0:T(8,128)S(1)} %get-tuple-element.33), channel_id=1, source_target_pairs={{0,6},{1,193},{2,0},{3,195},{4,2},{5,197},{6,4},{7,199},{8,14},{9,... | collective-permute-start | bytes 589832 | tf_op jit(solution)/shard_map/ppermute | solution.py:47
  77.2 6.8 %collective-permute-start.10 = (f32[384,128]{1,0:T(8,128)S(1)}, f32[384,128]{1,0:T(8,128)S(1)}, u32[]{:S(2)}, u32[]{:S(2)}) collective-permute-start(f32[384,128]{1,0:T(8,128)S(1)} %bitcast.122), channel_id=1, source_target_pairs={{0,2},{1,65},{2,4},{3,67},{4,6},{5,69},{6,0},{7,71},{8,10},{9,73},... | collective-permute-start | bytes 589832 | tf_op jit(solution)/shard_map/ppermute | solution.py:47
  78.5 8.8 %collective-permute-start.11 = (f32[384,128]{1,0:T(8,128)S(1)}, f32[384,128]{1,0:T(8,128)S(1)}, u32[]{:S(2)}, u32[]{:S(2)}) collective-permute-start(f32[384,128]{1,0:T(8,128)S(1)} %bitcast.123), channel_id=1, source_target_pairs={{0,4},{1,129},{2,6},{3,131},{4,0},{5,133},{6,2},{7,135},{8,12},{9,... | collective-permute-start | bytes 589832 | tf_op jit(solution)/shard_map/ppermute | solution.py:47
  82.1 5.2 %collective-permute-start.12 = (f32[384,128]{1,0:T(8,128)S(1)}, f32[384,128]{1,0:T(8,128)S(1)}, u32[]{:S(2)}, u32[]{:S(2)}) collective-permute-start(f32[384,128]{1,0:T(8,128)S(1)} %bitcast.124), channel_id=1, source_target_pairs={{0,6},{1,193},{2,0},{3,195},{4,2},{5,197},{6,4},{7,199},{8,14},{9,... | collective-permute-start | bytes 589832 | tf_op jit(solution)/shard_map/ppermute | solution.py:47
  87.9 22.9 %collective-permute-start.14 = (f32[1536,128]{1,0:T(8,128)S(1)}, f32[1536,128]{1,0:T(8,128)S(1)}, u32[]{:S(2)}, u32[]{:S(2)}) collective-permute-start(f32[1536,128]{1,0:T(8,128)S(1)} %join_quarter.1.refs_0_), channel_id=1, source_target_pairs={{0,64},{1,3},{2,66},{3,5},{4,68},{5,7},{6,70},{7,1},{8,72},{9,11},... | collective-permute-start | bytes 2359304 | tf_op jit(solution)/shard_map/ppermute | solution.py:41
  88.0 30.8 %collective-permute-start.16 = (f32[1536,128]{1,0:T(8,128)S(1)}, f32[1536,128]{1,0:T(8,128)S(1)}, u32[]{:S(2)}, u32[]{:S(2)}) collective-permute-start(f32[1536,128]{1,0:T(8,128)S(1)} %join_quarter.1.refs_0_), channel_id=1, source_target_pairs={{0,192},{1,7},{2,194},{3,1},{4,196},{5,3},{6,198},{7,5},{8,200},{9... | collective-permute-start | bytes 2359304 | tf_op jit(solution)/shard_map/ppermute | solution.py:41
  90.6 28.1 %collective-permute-start.18 = (f32[1536,128]{1,0:T(8,128)S(1)}, f32[1536,128]{1,0:T(8,128)S(1)}, u32[]{:S(2)}, u32[]{:S(2)}) collective-permute-start(f32[1536,128]{1,0:T(8,128)S(1)} %join_quarter.1.refs_0_), channel_id=1, source_target_pairs={{0,128},{1,5},{2,130},{3,7},{4,132},{5,1},{6,134},{7,3},{8,136},{9... | collective-permute-start | bytes 2359304 | tf_op jit(solution)/shard_map/ppermute | solution.py:41
  90.6 30.5 %collective-permute-start.13 = (f32[1536,128]{1,0:T(8,128)S(1)}, f32[1536,128]{1,0:T(8,128)S(1)}, u32[]{:S(2)}, u32[]{:S(2)}) collective-permute-start(f32[1536,128]{1,0:T(8,128)S(1)} %join_quarter.1.refs_0_), channel_id=1, source_target_pairs={{0,1},{1,0},{2,3},{3,2},{4,5},{5,4},{6,7},{7,6},{8,9},{9,8},{10,11... | collective-permute-start | bytes 2359304 | tf_op jit(solution)/shard_map/ppermute | solution.py:35
  110.8 12.1 %collective-permute-start.15 = (f32[1536,128]{1,0:T(8,128)S(1)}, f32[1536,128]{1,0:T(8,128)S(1)}, u32[]{:S(2)}, u32[]{:S(2)}) collective-permute-start(f32[1536,128]{1,0:T(8,128)S(1)} %collective-permute-done.14.refs_0_), channel_id=1, source_target_pairs={{0,1},{1,0},{2,3},{3,2},{4,5},{5,4},{6,7},{7,6},{8,9},{9,8},{10,11... | collective-permute-start | bytes 2359304 | tf_op jit(solution)/shard_map/ppermute | solution.py:35
  118.7 6.7 %collective-permute-start.17 = (f32[1536,128]{1,0:T(8,128)S(1)}, f32[1536,128]{1,0:T(8,128)S(1)}, u32[]{:S(2)}, u32[]{:S(2)}) collective-permute-start(f32[1536,128]{1,0:T(8,128)S(1)} %collective-permute-done.16.refs_0_), channel_id=1, source_target_pairs={{0,1},{1,0},{2,3},{3,2},{4,5},{5,4},{6,7},{7,6},{8,9},{9,8},{10,11... | collective-permute-start | bytes 2359304 | tf_op jit(solution)/shard_map/ppermute | solution.py:35
  118.7 9.2 %collective-permute-start.19 = (f32[1536,128]{1,0:T(8,128)S(1)}, f32[1536,128]{1,0:T(8,128)S(1)}, u32[]{:S(2)}, u32[]{:S(2)}) collective-permute-start(f32[1536,128]{1,0:T(8,128)S(1)} %collective-permute-done.18.refs_0_), channel_id=1, source_target_pairs={{0,1},{1,0},{2,3},{3,2},{4,5},{5,4},{6,7},{7,6},{8,9},{9,8},{10,11... | collective-permute-start | bytes 2359304 | tf_op jit(solution)/shard_map/ppermute | solution.py:35
  133.6 4.5 %collective-permute-start.21 = (f32[2,40,128]{2,1,0:T(8,128)S(1)}, f32[2,40,128]{2,1,0:T(8,128)S(1)}, u32[]{:S(2)}, u32[]{:S(2)}) collective-permute-start(f32[2,40,128]{2,1,0:T(8,128)S(1)} %pad_maximum_fusion), channel_id=1, source_target_pairs={{0,128},{1,5},{2,130},{3,7},{4,132},{5,1},{6,134},{7,3},{8,136},{9... | collective-permute-start | bytes 122888 | tf_op jit(solution)/shard_map/ppermute | solution.py:41
  133.8 4.8 %collective-permute-start.22 = (f32[2,40,128]{2,1,0:T(8,128)S(1)}, f32[2,40,128]{2,1,0:T(8,128)S(1)}, u32[]{:S(2)}, u32[]{:S(2)}) collective-permute-start(f32[2,40,128]{2,1,0:T(8,128)S(1)} %pad_maximum_fusion), channel_id=1, source_target_pairs={{0,64},{1,3},{2,66},{3,5},{4,68},{5,7},{6,70},{7,1},{8,72},{9,11},... | collective-permute-start | bytes 122888 | tf_op jit(solution)/shard_map/ppermute | solution.py:41
  133.8 4.8 %collective-permute-start.23 = (f32[2,40,128]{2,1,0:T(8,128)S(1)}, f32[2,40,128]{2,1,0:T(8,128)S(1)}, u32[]{:S(2)}, u32[]{:S(2)}) collective-permute-start(f32[2,40,128]{2,1,0:T(8,128)S(1)} %pad_maximum_fusion), channel_id=1, source_target_pairs={{0,192},{1,7},{2,194},{3,1},{4,196},{5,3},{6,198},{7,5},{8,200},{9... | collective-permute-start | bytes 122888 | tf_op jit(solution)/shard_map/ppermute | solution.py:41
  138.6 4.5 %collective-permute-start.24 = (f32[2,40,128]{2,1,0:T(8,128)S(1)}, f32[2,40,128]{2,1,0:T(8,128)S(1)}, u32[]{:S(2)}, u32[]{:S(2)}) collective-permute-start(f32[2,40,128]{2,1,0:T(8,128)S(1)} %pad_maximum_fusion.1), channel_id=1, source_target_pairs={{0,4},{1,129},{2,6},{3,131},{4,0},{5,133},{6,2},{7,135},{8,12},{9,... | collective-permute-start | bytes 122888 | tf_op jit(solution)/shard_map/ppermute | solution.py:47
  138.7 4.6 %collective-permute-start.25 = (f32[2,40,128]{2,1,0:T(8,128)S(1)}, f32[2,40,128]{2,1,0:T(8,128)S(1)}, u32[]{:S(2)}, u32[]{:S(2)}) collective-permute-start(f32[2,40,128]{2,1,0:T(8,128)S(1)} %pad_maximum_fusion.1), channel_id=1, source_target_pairs={{0,2},{1,65},{2,4},{3,67},{4,6},{5,69},{6,0},{7,71},{8,10},{9,73},... | collective-permute-start | bytes 122888 | tf_op jit(solution)/shard_map/ppermute | solution.py:47
  157.0 5.5 %collective-permute-start.27 = (f32[2,40,128]{2,1,0:T(8,128)S(1)}, f32[2,40,128]{2,1,0:T(8,128)S(1)}, u32[]{:S(2)}, u32[]{:S(2)}) collective-permute-start(f32[2,40,128]{2,1,0:T(8,128)S(1)} %pad_maximum_fusion.3.half_ref), channel_id=1, source_target_pairs={{0,1},{1,0},{2,3},{3,2},{4,5},{5,4},{6,7},{7,6},{8,9},{9,8},{10,11... | collective-permute-start | bytes 122888 | tf_op jit(solution)/shard_map/ppermute | solution.py:35
  (5 other events, 16.9 us)
where the time goes:
time: 179 us
  starting transfers between devices  48.1 us (27%)
  waiting for transfers between devices  45.4 us (25%)
  Pallas kernels  42 us (23%)
  blocking collectives  40.2 us (22%)
    ppermute x9, waiting for transfers between devices, first(): return lax.ppermute(value, AXES, pair_list(self.sizes, move))  32.3 us
    ppermute x10, starting transfers between devices, core(): lax.ppermute(value, AXES, pair_list(self.sizes, lambda x, z, y, c: (x, z,...  27.1 us
    all_to_all x1, blocking collectives, body(): own = lax.all_to_all(small, 'z', 0, 0)  16.7 us
    pallas_call x1, Pallas kernels, two_factors(): pl.pallas_call(functools.partial(factor_kernel, math.sqrt(total_snps), fl...  14.8 us
    ppermute x9, starting transfers between devices, second(): return lax.ppermute(value, AXES, pair_list(self.sizes, move))  13.1 us
    all_to_all x1, blocking collectives, sum_square(): lax.all_to_all(jnp.broadcast_to(half, (depth, *half.shape)), 'z', 0, 0)  12.4 us
    ppermute x9, waiting for transfers between devices, second(): return lax.ppermute(value, AXES, pair_list(self.sizes, move))  11.1 us
    pallas_call x5, Pallas kernels, range_piece(): pl.pallas_call(functools.partial(range_kernel, slots), in_specs=[SCALARS]...  11.1 us
  transfers between devices with their start and end apart: 28, of which 15 were waited for; matrix products, arithmetic and copies ran while one was open for 0% of the time, Pallas kernels for 8%

commit v1 on v0

--- a/solution.py
+++ b/solution.py
@@ -271,7 +271,7 @@
     )(table, half, other)
 
 
-STEPS = 3
+STEPS = 2
 CHUNKS = 16
 
 
@@ -402,16 +402,15 @@
     )(table, held, stats, probes)
 
 
-def range_kernel(slots, table_ref, held_ref, stats_ref, acc_ref, *refs):
-    *sketch_refs, out_ref = refs
+def range_kernel(k, table_ref, held_ref, stats_ref, mine_ref, theirs_ref, acc_ref, out_ref):
     width = acc_ref.shape[0]
-    whole = sketch_refs[0].shape[0]
+    whole = mine_ref.shape[0]
     rows = whole // STEPS
     out_ref[...] = acc_ref[...]
 
     def step(i, carry):
         part = pl.ds(pl.multiple_of(i * rows, rows), rows)
-        for slot, sketch_ref in zip(slots, sketch_refs):
+        for slot, sketch_ref in ((k, mine_ref), (4 + k, theirs_ref)):
             sketch = sketch_ref[part, :].T
             high = sketch.astype(jnp.bfloat16)
             rest = sketch - high.astype(jnp.float32)
@@ -426,21 +425,20 @@
     lax.fori_loop(0, STEPS, step, 0)
 
 
-def range_piece(slots, table, held, stats, acc, *sketches):
+def range_piece(k, table, held, stats, mine, theirs, acc):
     samples, snps = held.shape
-    width = acc.shape[0]
-    part = samples // 8 * len(slots)
-    return pl.pallas_call(
-        functools.partial(range_kernel, slots),
-        in_specs=[SCALARS] + [ONCHIP] * (3 + len(slots)),
+    width = mine.shape[1]
+    return pl.pallas_call(
+        functools.partial(range_kernel, (4 - k) % 4),
+        in_specs=[SCALARS] + [ONCHIP] * 5,
         out_specs=ONCHIP,
         out_shape=resident((width, snps)),
         compiler_params=LIMIT,
         cost_estimate=pl.CostEstimate(
-            flops=6 * part * snps * width, transcendentals=0, bytes_accessed=2 * part * snps
+            flops=3 * samples // 2 * snps * width, transcendentals=0, bytes_accessed=samples * snps // 2
         ),
         name="range_piece",
-    )(table, held, stats, acc, *(onchip(sketch) for sketch in sketches))
+    )(table, held, stats, onchip(mine), onchip(theirs), acc)
 
 
 def solution(mesh):
@@ -482,14 +480,9 @@
         for k in (1, 3, 2):
             mine[k] = torus.first(quarter, k)
         acc = jnp.zeros((width, snps), jnp.float32)
-        acc = range_piece((0,), table, held, stats, acc, quarter)
         for k in (0, 1, 3, 2):
-            slot = (4 - k) % 4
             theirs = torus.core(mine[k])
-            if k:
-                acc = range_piece((slot, 4 + slot), table, held, stats, acc, mine[k], theirs)
-            else:
-                acc = range_piece((4,), table, held, stats, acc, theirs)
+            acc = range_piece(k, table, held, stats, mine[k], theirs, acc)
         half, other = sum_square(torus, *local_gram(table, acc))
         basis, range_log_norms = two_factors(table, half, other, total_snps)
         unit_basis = lax.dot_general(

time: 179 us -> 176 us (0.983)
  Pallas kernels: 42 us -> 39.4 us
    pallas_call x5 -> x4, Pallas kernels: 11.1 us -> 9.19 us  [range_piece(): pl.pallas_call(functools.partial(range_kernel, (4 - k) % 4), in_specs=[SC...]
  transfers between devices with their start and end apart: 28 -> 28, of which waited for: 15 -> 15; matrix products, arithmetic and copies ran while one was open for 0% -> 0% of each run, Pallas kernels for 8% -> 7%
where the time goes in v1:
time: 176 us
  starting transfers between devices  48 us (27%)
  waiting for transfers between devices  45.4 us (26%)
  blocking collectives  40.2 us (23%)
  Pallas kernels  39.4 us (22%)
    ppermute x9, waiting for transfers between devices, first(): return lax.ppermute(value, AXES, pair_list(self.sizes, move))  32.3 us
    ppermute x10, starting transfers between devices, core(): lax.ppermute(value, AXES, pair_list(self.sizes, lambda x, z, y, c: (x, z,...  26.9 us
    all_to_all x1, blocking collectives, body(): own = lax.all_to_all(small, 'z', 0, 0)  16.7 us
    pallas_call x1, Pallas kernels, two_factors(): pl.pallas_call(functools.partial(factor_kernel, math.sqrt(total_snps), fl...  14.8 us
    ppermute x9, starting transfers between devices, second(): return lax.ppermute(value, AXES, pair_list(self.sizes, move))  13.1 us
    all_to_all x1, blocking collectives, sum_square(): lax.all_to_all(jnp.broadcast_to(half, (depth, *half.shape)), 'z', 0, 0)  12.4 us
    ppermute x9, waiting for transfers between devices, second(): return lax.ppermute(value, AXES, pair_list(self.sizes, move))  11.1 us
    all_to_all x1, blocking collectives, body(): small = lax.all_to_all(jnp.broadcast_to(own, (nz, *own.shape)), 'z', 0, 0)  11 us
  transfers between devices with their start and end apart: 28, of which 15 were waited for; matrix products, arithmetic and copies ran while one was open for 0% of the time, Pallas kernels for 7%

profile of v1, /device:TPU:1, one launch (start us, length us, event | category | flops | bytes accessed | tf_op | source)
XLA Modules:
  0.0 176.0 jit_solution(11007514937258877259)
XLA Ops:
  0.8 5.4 %dosage_stats.1 = (bf16[12288,512]{1,0:T(8,128)(2,1)S(1)}, f32[2,512]{1,0:T(2,128)S(1)}) custom-call(s32[13]{0:T(128)S(1)} %pad_add_fusion.table_ref, bf16[12288,512]{1,0:T(8,128)(2,1)} %source_ref.1), custom_call_target="tpu_custom_call" | custom-call | tf_op jit(solution)/shard_map/dosage_stats/pallas_call | solution.py:320
  7.9 3.3 %collective-permute-start.5 = (f32[1536,128]{1,0:T(8,128)S(1)}, f32[1536,128]{1,0:T(8,128)S(1)}, u32[]{:S(2)}, u32[]{:S(2)}) collective-permute-start(f32[1536,128]{1,0:T(8,128)S(1)} %get-tuple-element.29), channel_id=1, source_target_pairs={{0,1},{1,0},{2,3},{3,2},{4,5},{5,4},{6,7},{7,6},{8,9},{9,8},{10,11... | collective-permute-start | bytes 2359304 | tf_op jit(solution)/shard_map/ppermute | solution.py:35
  19.8 8.6 %collective-permute-done.6.three_ref = f32[1536,128]{1,0:T(8,128)S(1)} collective-permute-done((f32[1536,128]{1,0:T(8,128)S(1)}, f32[1536,128]{1,0:T(8,128)S(1)}, u32[]{:S(2)}, u32[]{:S(2)}) %collective-permute-start.6) | collective-permute-done | bytes 786464 | tf_op jit(solution)/shard_map/ppermute | solution.py:41
  28.4 2.7 %collective-permute-done.4.two_ref = f32[1536,128]{1,0:T(8,128)S(1)} collective-permute-done((f32[1536,128]{1,0:T(8,128)S(1)}, f32[1536,128]{1,0:T(8,128)S(1)}, u32[]{:S(2)}, u32[]{:S(2)}) %collective-permute-start.4) | collective-permute-done | bytes 786464 | tf_op jit(solution)/shard_map/ppermute | solution.py:41
  31.2 8.4 %collective-permute-done.2.one_ref = f32[1536,128]{1,0:T(8,128)S(1)} collective-permute-done((f32[1536,128]{1,0:T(8,128)S(1)}, f32[1536,128]{1,0:T(8,128)S(1)}, u32[]{:S(2)}, u32[]{:S(2)}) %collective-permute-start.2) | collective-permute-done | bytes 786464 | tf_op jit(solution)/shard_map/ppermute | solution.py:41
  40.3 2.5 %collective-permute-start.7 = (f32[384,128]{1,0:T(8,128)S(1)}, f32[384,128]{1,0:T(8,128)S(1)}, u32[]{:S(2)}, u32[]{:S(2)}) collective-permute-start(f32[384,128]{1,0:T(8,128)S(1)} %get-tuple-element.31), channel_id=1, source_target_pairs={{0,4},{1,129},{2,6},{3,131},{4,0},{5,133},{6,2},{7,135},{8,12},{9,... | collective-permute-start | bytes 589832 | tf_op jit(solution)/shard_map/ppermute | solution.py:47
  43.2 2.4 %collective-permute-start.9 = (f32[384,128]{1,0:T(8,128)S(1)}, f32[384,128]{1,0:T(8,128)S(1)}, u32[]{:S(2)}, u32[]{:S(2)}) collective-permute-start(f32[384,128]{1,0:T(8,128)S(1)} %get-tuple-element.33), channel_id=1, source_target_pairs={{0,6},{1,193},{2,0},{3,195},{4,2},{5,197},{6,4},{7,199},{8,14},{9,... | collective-permute-start | bytes 589832 | tf_op jit(solution)/shard_map/ppermute | solution.py:47
  48.6 16.7 %all_to_all.15 = f32[8,48,128]{2,1,0:T(8,128)S(1)} all-to-all(f32[8,48,128]{2,1,0:T(8,128)S(1)} %bitcast.126), channel_id=1, replica_groups=mesh['x'=4,'z'=8,'y'=4,'c'=2] {'z'}, dimensions={0} | all-to-all | bytes 393216 | tf_op jit(solution)/shard_map/all_to_all | solution.py:474
  65.4 11.0 %all_to_all.16 = f32[8,48,128]{2,1,0:T(8,128)S(1)} all-to-all(f32[8,48,128]{2,1,0:T(8,128)S(1)} %broadcast_in_dim.13), channel_id=1, replica_groups=mesh['x'=4,'z'=8,'y'=4,'c'=2] {'z'}, dimensions={0} | all-to-all | bytes 393216 | tf_op jit(solution)/shard_map/all_to_all | solution.py:476
  77.7 3.6 %collective-permute-start.11 = (f32[384,128]{1,0:T(8,128)S(1)}, f32[384,128]{1,0:T(8,128)S(1)}, u32[]{:S(2)}, u32[]{:S(2)}) collective-permute-start(f32[384,128]{1,0:T(8,128)S(1)} %bitcast.123), channel_id=1, source_target_pairs={{0,4},{1,129},{2,6},{3,131},{4,0},{5,133},{6,2},{7,135},{8,12},{9,... | collective-permute-start | bytes 589832 | tf_op jit(solution)/shard_map/ppermute | solution.py:47
  83.2 3.3 %collective-permute-done.11.refs_2_ = f32[384,128]{1,0:T(8,128)S(1)} collective-permute-done((f32[384,128]{1,0:T(8,128)S(1)}, f32[384,128]{1,0:T(8,128)S(1)}, u32[]{:S(2)}, u32[]{:S(2)}) %collective-permute-start.11) | collective-permute-done | bytes 196640 | tf_op jit(solution)/shard_map/ppermute | solution.py:47
  87.3 2.7 %collective-permute-start.15 = (f32[1536,128]{1,0:T(8,128)S(1)}, f32[1536,128]{1,0:T(8,128)S(1)}, u32[]{:S(2)}, u32[]{:S(2)}) collective-permute-start(f32[1536,128]{1,0:T(8,128)S(1)} %join_quarter.1.mine_ref), channel_id=1, source_target_pairs={{0,192},{1,7},{2,194},{3,1},{4,196},{5,3},{6,198},{7,5},{8,200},{9... | collective-permute-start | bytes 2359304 | tf_op jit(solution)/shard_map/ppermute | solution.py:41
  90.0 9.5 %collective-permute-start.19 = (f32[1536,128]{1,0:T(8,128)S(1)}, f32[1536,128]{1,0:T(8,128)S(1)}, u32[]{:S(2)}, u32[]{:S(2)}) collective-permute-start(f32[1536,128]{1,0:T(8,128)S(1)} %join_quarter.1.mine_ref), channel_id=1, source_target_pairs={{0,1},{1,0},{2,3},{3,2},{4,5},{5,4},{6,7},{7,6},{8,9},{9,8},{10,11... | collective-permute-start | bytes 2359304 | tf_op jit(solution)/shard_map/ppermute | solution.py:35
  99.5 10.4 %collective-permute-done.17.mine_ref = f32[1536,128]{1,0:T(8,128)S(1)} collective-permute-done((f32[1536,128]{1,0:T(8,128)S(1)}, f32[1536,128]{1,0:T(8,128)S(1)}, u32[]{:S(2)}, u32[]{:S(2)}) %collective-permute-start.17) | collective-permute-done | bytes 786464 | tf_op jit(solution)/shard_map/ppermute | solution.py:41
  110.0 7.9 %collective-permute-start.18 = (f32[1536,128]{1,0:T(8,128)S(1)}, f32[1536,128]{1,0:T(8,128)S(1)}, u32[]{:S(2)}, u32[]{:S(2)}) collective-permute-start(f32[1536,128]{1,0:T(8,128)S(1)} %collective-permute-done.17.mine_ref), channel_id=1, source_target_pairs={{0,1},{1,0},{2,3},{3,2},{4,5},{5,4},{6,7},{7,6},{8,9},{9,8},{10,11... | collective-permute-start | bytes 2359304 | tf_op jit(solution)/shard_map/ppermute | solution.py:35
  118.5 2.3 %range_piece.4.acc_ref = f32[128,512]{1,0:T(8,128)S(1)} custom-call(s32[13]{0:T(128)S(1)} %pad_add_fusion.table_ref, bf16[12288,512]{1,0:T(8,128)(2,1)S(1)} %get-tuple-element.20.held_ref, f32[2,512]{1,0:T(2,128)S(1)} %get-tuple-element.21.stats_ref, f32[1536,128]{1,0:T(8,128)S(1)} %join_quarter.1.mine_ref, ...), custom_call_target="tpu_custom_call" | custom-call | flops 1207959552 | bytes 3145728 | tf_op jit(solution)/shard_map/range_piece/pallas_call | solution.py:431
  120.8 2.3 %range_piece.5.acc_ref = f32[128,512]{1,0:T(8,128)S(1)} custom-call(s32[13]{0:T(128)S(1)} %pad_add_fusion.table_ref, bf16[12288,512]{1,0:T(8,128)(2,1)S(1)} %get-tuple-element.20.held_ref, f32[2,512]{1,0:T(2,128)S(1)} %get-tuple-element.21.stats_ref, f32[1536,128]{1,0:T(8,128)S(1)} %collective-permute-done.17.mine_ref, ...), custom_call_target="tpu_custom_call" | custom-call | flops 1207959552 | bytes 3145728 | tf_op jit(solution)/shard_map/range_piece/pallas_call | solution.py:431
  123.1 2.3 %range_piece.6.acc_ref = f32[128,512]{1,0:T(8,128)S(1)} custom-call(s32[13]{0:T(128)S(1)} %pad_add_fusion.table_ref, bf16[12288,512]{1,0:T(8,128)(2,1)S(1)} %get-tuple-element.20.held_ref, f32[2,512]{1,0:T(2,128)S(1)} %get-tuple-element.21.stats_ref, f32[1536,128]{1,0:T(8,128)S(1)} %collective-permute-done.15.mine_ref, ...), custom_call_target="tpu_custom_call" | custom-call | flops 1207959552 | bytes 3145728 | tf_op jit(solution)/shard_map/range_piece/pallas_call | solution.py:431
  125.4 2.3 %range_piece.7.range_ref = f32[128,512]{1,0:T(8,128)S(1)} custom-call(s32[13]{0:T(128)S(1)} %pad_add_fusion.table_ref, bf16[12288,512]{1,0:T(8,128)(2,1)S(1)} %get-tuple-element.20.held_ref, f32[2,512]{1,0:T(2,128)S(1)} %get-tuple-element.21.stats_ref, f32[1536,128]{1,0:T(8,128)S(1)} %collective-permute-done.13.mine_ref, ...), custom_call_target="tpu_custom_call" | custom-call | flops 1207959552 | bytes 3145728 | tf_op jit(solution)/shard_map/range_piece/pallas_call | solution.py:431
  131.1 2.7 %collective-permute-start.23 = (f32[2,40,128]{2,1,0:T(8,128)S(1)}, f32[2,40,128]{2,1,0:T(8,128)S(1)}, u32[]{:S(2)}, u32[]{:S(2)}) collective-permute-start(f32[2,40,128]{2,1,0:T(8,128)S(1)} %pad_maximum_fusion), channel_id=1, source_target_pairs={{0,192},{1,7},{2,194},{3,1},{4,196},{5,3},{6,198},{7,5},{8,200},{9... | collective-permute-start | bytes 122888 | tf_op jit(solution)/shard_map/ppermute | solution.py:41
  136.0 2.9 %collective-permute-start.25 = (f32[2,40,128]{2,1,0:T(8,128)S(1)}, f32[2,40,128]{2,1,0:T(8,128)S(1)}, u32[]{:S(2)}, u32[]{:S(2)}) collective-permute-start(f32[2,40,128]{2,1,0:T(8,128)S(1)} %pad_maximum_fusion.1), channel_id=1, source_target_pairs={{0,2},{1,65},{2,4},{3,67},{4,6},{5,69},{6,0},{7,71},{8,10},{9,73},... | collective-permute-start | bytes 122888 | tf_op jit(solution)/shard_map/ppermute | solution.py:47
  141.9 12.4 %all_to_all.17 = f32[8,2,40,128]{3,2,1,0:T(8,128)S(1)} all-to-all(f32[8,2,40,128]{3,2,1,0:T(8,128)S(1)} %broadcast_in_dim.15), channel_id=1, replica_groups=mesh['x'=4,'z'=8,'y'=4,'c'=2] {'z'}, dimensions={0} | all-to-all | bytes 655360 | tf_op jit(solution)/shard_map/all_to_all | solution.py:77
  154.4 4.6 %collective-permute-start.27 = (f32[2,40,128]{2,1,0:T(8,128)S(1)}, f32[2,40,128]{2,1,0:T(8,128)S(1)}, u32[]{:S(2)}, u32[]{:S(2)}) collective-permute-start(f32[2,40,128]{2,1,0:T(8,128)S(1)} %pad_maximum_fusion.3.half_ref), channel_id=1, source_target_pairs={{0,1},{1,0},{2,3},{3,2},{4,5},{5,4},{6,7},{7,6},{8,9},{9,8},{10,11... | collective-permute-start | bytes 122888 | tf_op jit(solution)/shard_map/ppermute | solution.py:35
  159.8 14.8 %two_factors.1 = (f32[128,128]{1,0:T(8,128)S(1)}, f32[1,128]{1,0:T(1,128)}) custom-call(s32[13]{0:T(128)S(1)} %pad_add_fusion.table_ref, f32[2,40,128]{2,1,0:T(8,128)S(1)} %pad_maximum_fusion.3.half_ref, f32[2,40,128]{2,1,0:T(8,128)S(1)} %collective-permute-done.27.other_ref), custom_call_target="tpu_custom_call" | custom-call | tf_op jit(solution)/shard_map/two_factors/pallas_call | solution.py:261
  (72 shorter events, 29.8 us)
Async XLA Ops:
  7.9 9.2 %collective-permute-start.5 = (f32[1536,128]{1,0:T(8,128)S(1)}, f32[1536,128]{1,0:T(8,128)S(1)}, u32[]{:S(2)}, u32[]{:S(2)}) collective-permute-start(f32[1536,128]{1,0:T(8,128)S(1)} %get-tuple-element.29), channel_id=1, source_target_pairs={{0,1},{1,0},{2,3},{3,2},{4,5},{5,4},{6,7},{7,6},{8,9},{9,8},{10,11... | collective-permute-start | bytes 2359304 | tf_op jit(solution)/shard_map/ppermute | solution.py:35
  12.9 5.4 %collective-permute-start.3 = (f32[1536,128]{1,0:T(8,128)S(1)}, f32[1536,128]{1,0:T(8,128)S(1)}, u32[]{:S(2)}, u32[]{:S(2)}) collective-permute-start(f32[1536,128]{1,0:T(8,128)S(1)} %get-tuple-element.27), channel_id=1, source_target_pairs={{0,1},{1,0},{2,3},{3,2},{4,5},{5,4},{6,7},{7,6},{8,9},{9,8},{10,11... | collective-permute-start | bytes 2359304 | tf_op jit(solution)/shard_map/ppermute | solution.py:35
  17.2 11.2 %collective-permute-start.6 = (f32[1536,128]{1,0:T(8,128)S(1)}, f32[1536,128]{1,0:T(8,128)S(1)}, u32[]{:S(2)}, u32[]{:S(2)}) collective-permute-start(f32[1536,128]{1,0:T(8,128)S(1)} %add.552), channel_id=1, source_target_pairs={{0,192},{1,7},{2,194},{3,1},{4,196},{5,3},{6,198},{7,5},{8,200},{9... | collective-permute-start | bytes 2359304 | tf_op jit(solution)/shard_map/ppermute | solution.py:41
  18.4 12.8 %collective-permute-start.4 = (f32[1536,128]{1,0:T(8,128)S(1)}, f32[1536,128]{1,0:T(8,128)S(1)}, u32[]{:S(2)}, u32[]{:S(2)}) collective-permute-start(f32[1536,128]{1,0:T(8,128)S(1)} %add.551), channel_id=1, source_target_pairs={{0,128},{1,5},{2,130},{3,7},{4,132},{5,1},{6,134},{7,3},{8,136},{9... | collective-permute-start | bytes 2359304 | tf_op jit(solution)/shard_map/ppermute | solution.py:41
  18.9 20.6 %collective-permute-start.2 = (f32[1536,128]{1,0:T(8,128)S(1)}, f32[1536,128]{1,0:T(8,128)S(1)}, u32[]{:S(2)}, u32[]{:S(2)}) collective-permute-start(f32[1536,128]{1,0:T(8,128)S(1)} %add.550), channel_id=1, source_target_pairs={{0,64},{1,3},{2,66},{3,5},{4,68},{5,7},{6,70},{7,1},{8,72},{9,11},... | collective-permute-start | bytes 2359304 | tf_op jit(solution)/shard_map/ppermute | solution.py:41
  40.3 6.4 %collective-permute-start.7 = (f32[384,128]{1,0:T(8,128)S(1)}, f32[384,128]{1,0:T(8,128)S(1)}, u32[]{:S(2)}, u32[]{:S(2)}) collective-permute-start(f32[384,128]{1,0:T(8,128)S(1)} %get-tuple-element.31), channel_id=1, source_target_pairs={{0,4},{1,129},{2,6},{3,131},{4,0},{5,133},{6,2},{7,135},{8,12},{9,... | collective-permute-start | bytes 589832 | tf_op jit(solution)/shard_map/ppermute | solution.py:47
  42.8 5.7 %collective-permute-start.8 = (f32[384,128]{1,0:T(8,128)S(1)}, f32[384,128]{1,0:T(8,128)S(1)}, u32[]{:S(2)}, u32[]{:S(2)}) collective-permute-start(f32[384,128]{1,0:T(8,128)S(1)} %get-tuple-element.32), channel_id=1, source_target_pairs={{0,2},{1,65},{2,4},{3,67},{4,6},{5,69},{6,0},{7,71},{8,10},{9,73},... | collective-permute-start | bytes 589832 | tf_op jit(solution)/shard_map/ppermute | solution.py:47
  43.2 5.4 %collective-permute-start.9 = (f32[384,128]{1,0:T(8,128)S(1)}, f32[384,128]{1,0:T(8,128)S(1)}, u32[]{:S(2)}, u32[]{:S(2)}) collective-permute-start(f32[384,128]{1,0:T(8,128)S(1)} %get-tuple-element.33), channel_id=1, source_target_pairs={{0,6},{1,193},{2,0},{3,195},{4,2},{5,197},{6,4},{7,199},{8,14},{9,... | collective-permute-start | bytes 589832 | tf_op jit(solution)/shard_map/ppermute | solution.py:47
  76.4 6.8 %collective-permute-start.10 = (f32[384,128]{1,0:T(8,128)S(1)}, f32[384,128]{1,0:T(8,128)S(1)}, u32[]{:S(2)}, u32[]{:S(2)}) collective-permute-start(f32[384,128]{1,0:T(8,128)S(1)} %bitcast.122), channel_id=1, source_target_pairs={{0,2},{1,65},{2,4},{3,67},{4,6},{5,69},{6,0},{7,71},{8,10},{9,73},... | collective-permute-start | bytes 589832 | tf_op jit(solution)/shard_map/ppermute | solution.py:47
  77.7 8.8 %collective-permute-start.11 = (f32[384,128]{1,0:T(8,128)S(1)}, f32[384,128]{1,0:T(8,128)S(1)}, u32[]{:S(2)}, u32[]{:S(2)}) collective-permute-start(f32[384,128]{1,0:T(8,128)S(1)} %bitcast.123), channel_id=1, source_target_pairs={{0,4},{1,129},{2,6},{3,131},{4,0},{5,133},{6,2},{7,135},{8,12},{9,... | collective-permute-start | bytes 589832 | tf_op jit(solution)/shard_map/ppermute | solution.py:47
  81.3 5.2 %collective-permute-start.12 = (f32[384,128]{1,0:T(8,128)S(1)}, f32[384,128]{1,0:T(8,128)S(1)}, u32[]{:S(2)}, u32[]{:S(2)}) collective-permute-start(f32[384,128]{1,0:T(8,128)S(1)} %bitcast.124), channel_id=1, source_target_pairs={{0,6},{1,193},{2,0},{3,195},{4,2},{5,197},{6,4},{7,199},{8,14},{9,... | collective-permute-start | bytes 589832 | tf_op jit(solution)/shard_map/ppermute | solution.py:47
  87.0 22.9 %collective-permute-start.17 = (f32[1536,128]{1,0:T(8,128)S(1)}, f32[1536,128]{1,0:T(8,128)S(1)}, u32[]{:S(2)}, u32[]{:S(2)}) collective-permute-start(f32[1536,128]{1,0:T(8,128)S(1)} %join_quarter.1.mine_ref), channel_id=1, source_target_pairs={{0,64},{1,3},{2,66},{3,5},{4,68},{5,7},{6,70},{7,1},{8,72},{9,11},... | collective-permute-start | bytes 2359304 | tf_op jit(solution)/shard_map/ppermute | solution.py:41
  87.3 30.6 %collective-permute-start.15 = (f32[1536,128]{1,0:T(8,128)S(1)}, f32[1536,128]{1,0:T(8,128)S(1)}, u32[]{:S(2)}, u32[]{:S(2)}) collective-permute-start(f32[1536,128]{1,0:T(8,128)S(1)} %join_quarter.1.mine_ref), channel_id=1, source_target_pairs={{0,192},{1,7},{2,194},{3,1},{4,196},{5,3},{6,198},{7,5},{8,200},{9... | collective-permute-start | bytes 2359304 | tf_op jit(solution)/shard_map/ppermute | solution.py:41
  90.0 27.9 %collective-permute-start.13 = (f32[1536,128]{1,0:T(8,128)S(1)}, f32[1536,128]{1,0:T(8,128)S(1)}, u32[]{:S(2)}, u32[]{:S(2)}) collective-permute-start(f32[1536,128]{1,0:T(8,128)S(1)} %join_quarter.1.mine_ref), channel_id=1, source_target_pairs={{0,128},{1,5},{2,130},{3,7},{4,132},{5,1},{6,134},{7,3},{8,136},{9... | collective-permute-start | bytes 2359304 | tf_op jit(solution)/shard_map/ppermute | solution.py:41
  90.0 28.5 %collective-permute-start.19 = (f32[1536,128]{1,0:T(8,128)S(1)}, f32[1536,128]{1,0:T(8,128)S(1)}, u32[]{:S(2)}, u32[]{:S(2)}) collective-permute-start(f32[1536,128]{1,0:T(8,128)S(1)} %join_quarter.1.mine_ref), channel_id=1, source_target_pairs={{0,1},{1,0},{2,3},{3,2},{4,5},{5,4},{6,7},{7,6},{8,9},{9,8},{10,11... | collective-permute-start | bytes 2359304 | tf_op jit(solution)/shard_map/ppermute | solution.py:35
  110.0 10.8 %collective-permute-start.18 = (f32[1536,128]{1,0:T(8,128)S(1)}, f32[1536,128]{1,0:T(8,128)S(1)}, u32[]{:S(2)}, u32[]{:S(2)}) collective-permute-start(f32[1536,128]{1,0:T(8,128)S(1)} %collective-permute-done.17.mine_ref), channel_id=1, source_target_pairs={{0,1},{1,0},{2,3},{3,2},{4,5},{5,4},{6,7},{7,6},{8,9},{9,8},{10,11... | collective-permute-start | bytes 2359304 | tf_op jit(solution)/shard_map/ppermute | solution.py:35
  117.9 5.2 %collective-permute-start.16 = (f32[1536,128]{1,0:T(8,128)S(1)}, f32[1536,128]{1,0:T(8,128)S(1)}, u32[]{:S(2)}, u32[]{:S(2)}) collective-permute-start(f32[1536,128]{1,0:T(8,128)S(1)} %collective-permute-done.15.mine_ref), channel_id=1, source_target_pairs={{0,1},{1,0},{2,3},{3,2},{4,5},{5,4},{6,7},{7,6},{8,9},{9,8},{10,11... | collective-permute-start | bytes 2359304 | tf_op jit(solution)/shard_map/ppermute | solution.py:35
  117.9 7.5 %collective-permute-start.14 = (f32[1536,128]{1,0:T(8,128)S(1)}, f32[1536,128]{1,0:T(8,128)S(1)}, u32[]{:S(2)}, u32[]{:S(2)}) collective-permute-start(f32[1536,128]{1,0:T(8,128)S(1)} %collective-permute-done.13.mine_ref), channel_id=1, source_target_pairs={{0,1},{1,0},{2,3},{3,2},{4,5},{5,4},{6,7},{7,6},{8,9},{9,8},{10,11... | collective-permute-start | bytes 2359304 | tf_op jit(solution)/shard_map/ppermute | solution.py:35
  130.9 4.5 %collective-permute-start.21 = (f32[2,40,128]{2,1,0:T(8,128)S(1)}, f32[2,40,128]{2,1,0:T(8,128)S(1)}, u32[]{:S(2)}, u32[]{:S(2)}) collective-permute-start(f32[2,40,128]{2,1,0:T(8,128)S(1)} %pad_maximum_fusion), channel_id=1, source_target_pairs={{0,128},{1,5},{2,130},{3,7},{4,132},{5,1},{6,134},{7,3},{8,136},{9... | collective-permute-start | bytes 122888 | tf_op jit(solution)/shard_map/ppermute | solution.py:41
  131.1 4.8 %collective-permute-start.22 = (f32[2,40,128]{2,1,0:T(8,128)S(1)}, f32[2,40,128]{2,1,0:T(8,128)S(1)}, u32[]{:S(2)}, u32[]{:S(2)}) collective-permute-start(f32[2,40,128]{2,1,0:T(8,128)S(1)} %pad_maximum_fusion), channel_id=1, source_target_pairs={{0,64},{1,3},{2,66},{3,5},{4,68},{5,7},{6,70},{7,1},{8,72},{9,11},... | collective-permute-start | bytes 122888 | tf_op jit(solution)/shard_map/ppermute | solution.py:41
  131.1 4.8 %collective-permute-start.23 = (f32[2,40,128]{2,1,0:T(8,128)S(1)}, f32[2,40,128]{2,1,0:T(8,128)S(1)}, u32[]{:S(2)}, u32[]{:S(2)}) collective-permute-start(f32[2,40,128]{2,1,0:T(8,128)S(1)} %pad_maximum_fusion), channel_id=1, source_target_pairs={{0,192},{1,7},{2,194},{3,1},{4,196},{5,3},{6,198},{7,5},{8,200},{9... | collective-permute-start | bytes 122888 | tf_op jit(solution)/shard_map/ppermute | solution.py:41
  135.9 4.5 %collective-permute-start.24 = (f32[2,40,128]{2,1,0:T(8,128)S(1)}, f32[2,40,128]{2,1,0:T(8,128)S(1)}, u32[]{:S(2)}, u32[]{:S(2)}) collective-permute-start(f32[2,40,128]{2,1,0:T(8,128)S(1)} %pad_maximum_fusion.1), channel_id=1, source_target_pairs={{0,4},{1,129},{2,6},{3,131},{4,0},{5,133},{6,2},{7,135},{8,12},{9,... | collective-permute-start | bytes 122888 | tf_op jit(solution)/shard_map/ppermute | solution.py:47
  136.0 4.6 %collective-permute-start.25 = (f32[2,40,128]{2,1,0:T(8,128)S(1)}, f32[2,40,128]{2,1,0:T(8,128)S(1)}, u32[]{:S(2)}, u32[]{:S(2)}) collective-permute-start(f32[2,40,128]{2,1,0:T(8,128)S(1)} %pad_maximum_fusion.1), channel_id=1, source_target_pairs={{0,2},{1,65},{2,4},{3,67},{4,6},{5,69},{6,0},{7,71},{8,10},{9,73},... | collective-permute-start | bytes 122888 | tf_op jit(solution)/shard_map/ppermute | solution.py:47
  154.4 5.5 %collective-permute-start.27 = (f32[2,40,128]{2,1,0:T(8,128)S(1)}, f32[2,40,128]{2,1,0:T(8,128)S(1)}, u32[]{:S(2)}, u32[]{:S(2)}) collective-permute-start(f32[2,40,128]{2,1,0:T(8,128)S(1)} %pad_maximum_fusion.3.half_ref), channel_id=1, source_target_pairs={{0,1},{1,0},{2,3},{3,2},{4,5},{5,4},{6,7},{7,6},{8,9},{9,8},{10,11... | collective-permute-start | bytes 122888 | tf_op jit(solution)/shard_map/ppermute | solution.py:35
  (5 other events, 16.5 us)
